TPU v7x, 32 devices: a whole 2x2x4 slice. The times are simulated.
32 devices in a mesh: dp: 2 (over core), ctx: 4 (over y, x), hd: 4 (over z).
Axes of the slice: x: 2, y: 2, z: 4, core: 2. Of those that a mesh axis runs over, the one named last changes fastest.
Arguments:
- tokens_in: bfloat16 [4, 2048, 1536], P('dp', ('ctx', 'hd')), may hold values from -6 to 6
- seg_ids: int32 [4, 2048], P('dp'), may hold values from 0 to 7, never falling along the last dimension, each value on 1 to 512 neighbouring positions
- in_norm: float32 [1536], replicated, may hold values from 0.5 to 1.5
- z_proj: bfloat16 [1536, 3072], P(('dp', 'ctx', 'hd')), may hold values from -0.15625 to 0.15625
- xbc_proj: bfloat16 [1536, 3328], P(('dp', 'ctx', 'hd')), may hold values from -0.15625 to 0.15625
- dt_proj: bfloat16 [1536, 48], P(('dp', 'ctx', 'hd')), may hold values from -0.0390625 to 0.0390625
- conv_taps: float32 [4, 3328], replicated, may hold values from -3 to 3
- conv_bias: float32 [3328], replicated, may hold values from -2 to 2
- dt_bias: float32 [48], replicated, may hold values from -9 to -2
- a_log: float32 [48], replicated, may hold values from 0 to 2.77
- d_skip: float32 [48], replicated, may hold values from 0.5 to 2
- gate_norm: float32 [3072], replicated, may hold values from 0.5 to 1.5
- out_proj: bfloat16 [3072, 1536], P(('dp', 'ctx', 'hd')), may hold values from -0.109375 to 0.109375
- out_cotangent: bfloat16 [4, 2048, 1536], P('dp', ('ctx', 'hd')), may hold values from -6 to 6
Outputs:
- layer_out: bfloat16 [4, 2048, 1536], P('dp', ('ctx', 'hd'))
- tokens_grad: float32 [4, 2048, 1536], P('dp', ('ctx', 'hd'))
- in_norm_grad: float32 [1536], replicated
- z_proj_grad: float32 [1536, 3072], P(('dp', 'ctx', 'hd'))
- xbc_proj_grad: float32 [1536, 3328], P(('dp', 'ctx', 'hd'))
- dt_proj_grad: float32 [1536, 48], P(('dp', 'ctx', 'hd'))
- conv_taps_grad: float32 [4, 3328], replicated
- conv_bias_grad: float32 [3328], replicated
- dt_bias_grad: float32 [48], replicated
- a_log_grad: float32 [48], replicated
- d_skip_grad: float32 [48], replicated
- gate_norm_grad: float32 [3072], replicated
- out_proj_grad: float32 [3072, 1536], P(('dp', 'ctx', 'hd'))
Inputs may be any that keep to these rules, and one draw needn't show every extreme that they name: `seg_ids`: along each sequence the document numbers never fall; each document has 1 to 512 tokens and one has exactly that many.
All inputs are finite; a program needn't handle non-finite values.
Results may differ from a plain program's by a relative error of at most 0.0097.
Values may be sent and summed in bfloat16 or wider, within the bound.
No kernel may reach another device: no remote copies, remote signals or barrier semaphores. Data moves between devices by JAX's collectives and lax.ppermute only.
A program may use at most 320 MiB of HBM per device.

v0:
```python
import jax
import jax.numpy as jnp
from jax import lax
from jax.sharding import PartitionSpec as P

H = 48
P_SIZE = 64
N = 128
KW = 4
Q = 256
DI = 3072
HIGH = lax.Precision.HIGHEST
EPS = 1e-05


def from_behind(shard, axis, by):
    count = lax.axis_size(axis)
    pairs = [(i, i + by) for i in range(count) if 0 <= i + by < count]
    return lax.ppermute(shard, axis, pairs)


def carried_in(shard, axis, combine, identity, reverse):
    count, place = (lax.axis_size(axis), lax.axis_index(axis))
    everything = jax.tree.map(
        lambda part, kind: lax.all_gather(part.astype(kind), axis),
        shard,
        (jnp.bfloat16, jnp.bfloat16),
    )
    start = jax.tree.map(
        lambda part, zero: jnp.broadcast_to(jnp.asarray(zero, part.dtype), part.shape),
        shard,
        identity,
    )

    def turn(k, before):
        at = count - 1 - k if reverse else k
        reached = at > place if reverse else at < place
        new = combine(
            before, jax.tree.map(lambda part, own: part[at].astype(own.dtype), everything, shard)
        )
        return jax.tree.map(lambda a, b: jnp.where(reached, a, b), new, before)

    return lax.fori_loop(0, count, turn, start)


def norm_rows(values, gain):
    return values * lax.rsqrt(jnp.mean(values * values, axis=-1, keepdims=True) + EPS) * gain


def gate_tail(mixer_val, gate_val, gain):
    return norm_rows(mixer_val * jax.nn.silu(gate_val), gain)


def conv_act(padded, taps, bias, masks):
    length = masks.shape[1]
    mixed = bias
    for tap in range(taps.shape[0]):
        mixed = mixed + taps[tap] * padded[tap : tap + length] * masks[tap][:, None]
    return jax.nn.silu(mixed)


def back_dot(grad_val, weight):
    return lax.dot_general(
        grad_val, weight, (((1,), (1,)), ((), ())), preferred_element_type=jnp.float32
    )


def compose(earlier, later):
    return (earlier[0] * later[0], later[0][:, None, None] * earlier[1] + later[1])


def block_decay(rate_val, bias_here, decay_log, seg_blk, seg_before):
    log_rate = jax.nn.softplus(rate_val + bias_here) * -jnp.exp(decay_log)
    cumul = jnp.cumsum(log_rate, axis=0)
    keep = (seg_blk == seg_before).astype(jnp.float32)
    lead = jnp.exp(cumul) * keep[:, None]
    return (lead[-1], lead)


def block_ssd(
    x_val,
    rate_val,
    bias_here,
    decay_log,
    skip_here,
    bc_val,
    state_in,
    seg_blk,
    seg_before,
    span_len,
):
    length, heads = rate_val.shape
    count = length // span_len
    width_n = bc_val.shape[1] // 2
    x_groups = x_val.reshape(count, span_len, heads, -1)
    dt_groups = jax.nn.softplus(rate_val + bias_here).reshape(count, span_len, heads)
    cumul = jnp.cumsum(dt_groups * -jnp.exp(decay_log), axis=1)
    b_groups = bc_val[:, :width_n].reshape(count, span_len, width_n)
    c_groups = bc_val[:, width_n:].reshape(count, span_len, width_n)
    seg_groups = seg_blk.reshape(count, span_len)
    before = jnp.concatenate([seg_before, seg_groups[:-1, -1]])
    order = jnp.arange(span_len)
    mask = (seg_groups[:, :, None] == seg_groups[:, None, :]) & (order[:, None] >= order[None, :])
    gaps = cumul[:, :, None, :] - cumul[:, None, :, :]
    decay = jnp.exp(jnp.where(mask[..., None], gaps, 0.0)) * mask[..., None].astype(jnp.float32)
    scores = jnp.einsum("ctn,csn->cts", c_groups, b_groups, precision=HIGH)
    mix_w = scores[..., None] * decay * dt_groups[:, None, :, :]
    y_part = jnp.einsum("ctsh,cshp->cthp", mix_w, x_groups, precision=HIGH)
    keep = (seg_groups == before[:, None]).astype(jnp.float32)
    lead = jnp.exp(cumul) * keep[..., None]
    tail = (
        jnp.exp(cumul[:, -1:, :] - cumul)
        * (seg_groups == seg_groups[:, -1:]).astype(jnp.float32)[..., None]
        * dt_groups
    )
    pieces = jnp.einsum("csh,cshp,csn->chpn", tail, x_groups, b_groups, precision=HIGH)

    def advance(state, item):
        piece, factor = item
        return (state * factor[:, None, None] + piece, state)

    state_end, entering = lax.scan(advance, state_in, (pieces, lead[:, -1, :]))
    y_part = y_part + lead[..., None] * jnp.einsum(
        "ctn,chpn->cthp", c_groups, entering, precision=HIGH
    )
    y_part = y_part + skip_here[:, None] * x_groups
    return (y_part.reshape(length, -1), state_end)


def shards(
    tokens_in,
    seg_ids,
    in_norm,
    z_proj,
    xbc_proj,
    dt_proj,
    conv_taps,
    conv_bias,
    dt_bias,
    a_log,
    d_skip,
    gate_norm,
    out_proj,
    out_cotangent,
):
    batches, rows, width = tokens_in.shape
    n_heads_axis = lax.axis_size("hd")
    heads_here = H // n_heads_axis
    block = rows * n_heads_axis
    channels = DI + 2 * N
    start_tok = lax.axis_index(("ctx", "hd")) * rows
    start_blk = lax.axis_index("ctx") * block
    head_low = lax.axis_index("hd") * heads_here
    bias_here = lax.dynamic_slice_in_dim(dt_bias, head_low, heads_here)
    decay_log = lax.dynamic_slice_in_dim(a_log, head_low, heads_here)
    skip_here = lax.dynamic_slice_in_dim(d_skip, head_low, heads_here)
    unit = (jnp.ones((heads_here,), jnp.float32), jnp.zeros((heads_here, P_SIZE, N), jnp.float32))

    def fetch():
        return (
            lax.all_gather(z_proj, ("dp", "ctx", "hd"), axis=0, tiled=True),
            lax.all_gather(xbc_proj, ("dp", "ctx", "hd"), axis=0, tiled=True),
            lax.all_gather(dt_proj, ("dp", "ctx", "hd"), axis=0, tiled=True),
            lax.all_gather(out_proj, ("dp", "ctx", "hd"), axis=0, tiled=True),
        )

    stored = []
    outputs = []
    for batch in range(batches):
        zed_weight, xbc_weight, rate_weight, out_weight = fetch()
        seg_row = seg_ids[batch]
        seg_pad = jnp.concatenate([jnp.full((KW - 1,), -1, jnp.int32), seg_row])
        seg_near = lax.dynamic_slice_in_dim(seg_pad, start_tok, rows + KW - 1)
        seg_own = seg_near[KW - 1 :]
        masks = jnp.stack([seg_near[tap : tap + rows] == seg_own for tap in range(KW)]).astype(
            jnp.float32
        )
        seg_blk = lax.dynamic_slice_in_dim(seg_row, start_blk, block)
        seg_before = lax.dynamic_slice_in_dim(seg_pad, start_blk + KW - 2, 1)
        source = tokens_in[batch].astype(jnp.float32)
        normed = norm_rows(source, in_norm).astype(jnp.bfloat16)
        gate_in = jnp.dot(normed, zed_weight, preferred_element_type=jnp.float32)
        raw_xbc = jnp.dot(normed, xbc_weight, preferred_element_type=jnp.float32).astype(
            jnp.bfloat16
        )
        rate_raw = jnp.dot(normed, rate_weight, preferred_element_type=jnp.float32).astype(
            jnp.bfloat16
        )
        rim_rows = from_behind(raw_xbc[rows - (KW - 1) :], ("ctx", "hd"), 1)
        padded = jnp.concatenate([rim_rows, raw_xbc], 0).astype(jnp.float32)
        active = conv_act(padded, conv_taps, conv_bias, masks)
        x_low = active[:, :DI].astype(jnp.bfloat16)
        bc_low = active[:, DI:].astype(jnp.bfloat16)
        x_heads, rate_heads = (
            lax.all_to_all(x_low, "hd", split_axis=1, concat_axis=0, tiled=True),
            lax.all_to_all(rate_raw, "hd", split_axis=1, concat_axis=0, tiled=True),
        )
        bc_all = lax.all_gather(bc_low, "hd", axis=0, tiled=True)
        x_float = x_heads.astype(jnp.float32)
        rate_float = rate_heads.astype(jnp.float32)
        bc_float = bc_all.astype(jnp.float32)
        zero_state = jnp.zeros((heads_here, P_SIZE, N), jnp.float32)
        y_zero, state_local = block_ssd(
            x_float,
            rate_float,
            bias_here,
            decay_log,
            skip_here,
            bc_float,
            zero_state,
            seg_blk,
            seg_before,
            Q,
        )
        total_decay, lead_blk = block_decay(rate_float, bias_here, decay_log, seg_blk, seg_before)
        unused, state_in = carried_in((total_decay, state_local), "ctx", compose, unit, False)
        carried = lead_blk[:, :, None] * jnp.einsum(
            "tn,hpn->thp", bc_float[:, N:], state_in, precision=HIGH
        )
        y_heads = y_zero + carried.reshape(block, -1)
        y_tokens = lax.all_to_all(
            y_heads.astype(jnp.bfloat16), "hd", split_axis=0, concat_axis=1, tiled=True
        )
        y_float = y_tokens.astype(jnp.float32)
        gated = gate_tail(y_float, gate_in, gate_norm).astype(jnp.bfloat16)
        result = source + jnp.dot(gated, out_weight, preferred_element_type=jnp.float32)
        outputs.append(result.astype(jnp.bfloat16))
        stored.append(
            (
                source,
                normed,
                gate_in,
                padded,
                masks,
                x_float,
                rate_float,
                bc_float,
                seg_blk,
                seg_before,
                lead_blk,
                total_decay,
                state_in,
                y_float,
                gated,
            )
        )
    grads_tok = []
    normed_rows = []
    proj_grads = []
    gated_rows = []
    cot_rows = []
    norm_total = jnp.zeros((width,), jnp.float32)
    taps_total = jnp.zeros(conv_taps.shape, jnp.float32)
    cbias_total = jnp.zeros((channels,), jnp.float32)
    dtb_total = jnp.zeros((H,), jnp.float32)
    alog_total = jnp.zeros((H,), jnp.float32)
    skip_total = jnp.zeros((H,), jnp.float32)
    gate_total = jnp.zeros((DI,), jnp.float32)
    for batch in range(batches):
        zed_weight, xbc_weight, rate_weight, out_weight = fetch()
        (
            source,
            normed,
            gate_in,
            padded,
            masks,
            x_float,
            rate_float,
            bc_float,
            seg_blk,
            seg_before,
            lead_blk,
            total_decay,
            state_in,
            y_float,
            gated,
        ) = stored[batch]
        cot_low = out_cotangent[batch]
        d_gated = back_dot(cot_low, out_weight)
        unused, tail_pull = jax.vjp(gate_tail, y_float, gate_in, gate_norm)
        d_mixer, d_gate_in, d_gain = tail_pull(d_gated)
        d_mixer_heads = lax.all_to_all(
            d_mixer.astype(jnp.bfloat16), "hd", split_axis=1, concat_axis=0, tiled=True
        )
        d_y_float = d_mixer_heads.astype(jnp.float32)
        d_local = jnp.einsum(
            "th,thp,tn->hpn",
            lead_blk,
            d_y_float.reshape(block, heads_here, P_SIZE),
            bc_float[:, N:],
            precision=HIGH,
        )
        unused, d_end = carried_in((total_decay, d_local), "ctx", compose, unit, True)

        def with_state(x_value, rate_value, bias_value, decay_value, skip_value, bc_value):
            return block_ssd(
                x_value,
                rate_value,
                bias_value,
                decay_value,
                skip_value,
                bc_value,
                state_in,
                seg_blk,
                seg_before,
                Q,
            )

        unused, ssd_pull = jax.vjp(
            with_state, x_float, rate_float, bias_here, decay_log, skip_here, bc_float
        )
        d_x_heads, d_rate_heads, d_bias_h, d_decay_h, d_skip_h, d_bc_heads = ssd_pull(
            (d_y_float, d_end)
        )
        d_x_tok, d_rate_tok = (
            lax.all_to_all(
                d_x_heads.astype(jnp.bfloat16), "hd", split_axis=0, concat_axis=1, tiled=True
            ),
            lax.all_to_all(
                d_rate_heads.astype(jnp.bfloat16), "hd", split_axis=0, concat_axis=1, tiled=True
            ),
        )
        d_bc_tok = lax.psum_scatter(
            d_bc_heads.astype(jnp.bfloat16), "hd", scatter_dimension=0, tiled=True
        ).astype(jnp.float32)
        d_active = jnp.concatenate([d_x_tok.astype(jnp.float32), d_bc_tok], axis=1)

        def conv_here(pad_value, taps_value, bias_value):
            return conv_act(pad_value, taps_value, bias_value, masks)

        unused, conv_pull = jax.vjp(conv_here, padded, conv_taps, conv_bias)
        d_padded, d_taps, d_cbias = conv_pull(d_active)
        back_rim = from_behind(d_padded[: KW - 1].astype(jnp.bfloat16), ("ctx", "hd"), -1).astype(
            jnp.float32
        )
        d_raw = d_padded[KW - 1 :] + jnp.concatenate(
            [jnp.zeros((rows - (KW - 1), channels), jnp.float32), back_rim], 0
        )
        d_raw_low = d_raw.astype(jnp.bfloat16)
        d_gate_low = d_gate_in.astype(jnp.bfloat16)
        d_normed = (
            back_dot(d_gate_low, zed_weight)
            + back_dot(d_raw_low, xbc_weight)
            + back_dot(d_rate_tok, rate_weight)
        )
        unused, norm_pull = jax.vjp(norm_rows, source, in_norm)
        d_source, d_norm_gain = norm_pull(d_normed)
        grads_tok.append(d_source + cot_low.astype(jnp.float32))
        normed_rows.append(normed)
        proj_grads.append(jnp.concatenate([d_gate_low, d_raw_low, d_rate_tok], axis=1))
        gated_rows.append(gated)
        cot_rows.append(cot_low)
        norm_total = norm_total + d_norm_gain
        taps_total = taps_total + d_taps
        cbias_total = cbias_total + d_cbias
        dtb_total = dtb_total + lax.dynamic_update_slice_in_dim(
            jnp.zeros((H,), jnp.float32), d_bias_h, head_low, 0
        )
        alog_total = alog_total + lax.dynamic_update_slice_in_dim(
            jnp.zeros((H,), jnp.float32), d_decay_h, head_low, 0
        )
        skip_total = skip_total + lax.dynamic_update_slice_in_dim(
            jnp.zeros((H,), jnp.float32), d_skip_h, head_low, 0
        )
        gate_total = gate_total + d_gain
    normed_all = jnp.concatenate(normed_rows, 0)
    proj_all = jnp.concatenate(proj_grads, 0)
    gated_all = jnp.concatenate(gated_rows, 0)
    cot_all = jnp.concatenate(cot_rows, 0)
    part = normed_all
    in_grad = lax.psum_scatter(
        lax.dot_general(
            part, proj_all, (((0,), (0,)), ((), ())), preferred_element_type=jnp.float32
        ),
        ("dp", "ctx", "hd"),
        scatter_dimension=0,
        tiled=True,
    )
    part = gated_all
    out_grad = lax.psum_scatter(
        lax.dot_general(
            part, cot_all, (((0,), (0,)), ((), ())), preferred_element_type=jnp.float32
        ),
        ("dp", "ctx", "hd"),
        scatter_dimension=0,
        tiled=True,
    )
    norm_sum, taps_sum, cbias_sum, dtb_sum, alog_sum, skip_sum, gate_sum = lax.psum(
        (norm_total, taps_total, cbias_total, dtb_total, alog_total, skip_total, gate_total),
        ("dp", "ctx", "hd"),
    )
    return (
        jnp.stack(outputs),
        jnp.stack(grads_tok),
        norm_sum,
        in_grad[:, :DI],
        in_grad[:, DI : DI + channels],
        in_grad[:, DI + channels :],
        taps_sum,
        cbias_sum,
        dtb_sum,
        alog_sum,
        skip_sum,
        gate_sum,
        out_grad,
    )


def solution(mesh):
    in_specs = (
        P("dp", ("ctx", "hd"), None),
        P("dp", None),
        P(),
        P(("dp", "ctx", "hd"), None),
        P(("dp", "ctx", "hd"), None),
        P(("dp", "ctx", "hd"), None),
        P(),
        P(),
        P(),
        P(),
        P(),
        P(),
        P(("dp", "ctx", "hd"), None),
        P("dp", ("ctx", "hd"), None),
    )
    out_specs = (
        P("dp", ("ctx", "hd"), None),
        P("dp", ("ctx", "hd"), None),
        P(),
        P(("dp", "ctx", "hd"), None),
        P(("dp", "ctx", "hd"), None),
        P(("dp", "ctx", "hd"), None),
        P(),
        P(),
        P(),
        P(),
        P(),
        P(),
        P(("dp", "ctx", "hd"), None),
    )
    return jax.shard_map(shards, mesh=mesh, in_specs=in_specs, out_specs=out_specs, check_vma=False)
```

profile of v0, /device:TPU:0, one launch (start us, length us, event | category | flops | bytes accessed | tf_op | source)
XLA Modules:
  0.0 1491.1 jit_solution(12795185626710274791)
XLA Ops:
  8.7 76.8 %all_gather.68 = bf16[1536,48]{1,0:T(8,128)(2,1)S(1)} all-gather(bf16[48,48]{1,0:T(8,128)(2,1)} %param.40), channel_id=1, replica_groups=mesh['dp'=2,'ctx'=4,'hd'=4] {'dp','ctx','hd'}, dimensions={0}, use_global_device_ids=true | all-gather | bytes 152064 | tf_op jit(solution)/shard_map/all_gather | solution.py:163
  110.2 5.7 all-to-all-done.1
  125.4 14.0 all-gather.5
  141.8 6.4 all-gather.4
  152.6 6.6 convolution_convert_fusion
  173.7 6.7 all-to-all-start.3
  188.7 17.7 %all_gather.74 = bf16[512,256]{1,0:T(8,128)(2,1)S(1)} all-gather(bf16[128,256]{1,0:T(8,128)(2,1)S(1)} %slice.403), channel_id=1, replica_groups=mesh['dp'=2,'ctx'=4,'hd'=4] {'hd'}, dimensions={0}, use_global_device_ids=true | all-gather | bytes 327680 | tf_op jit(solution)/shard_map/all_gather | solution.py:198
  206.4 15.0 %all_gather.33 = bf16[512,256]{1,0:T(8,128)(2,1)S(1)} all-gather(bf16[128,256]{1,0:T(8,128)(2,1)S(1)} %slice.386), channel_id=1, replica_groups=mesh['dp'=2,'ctx'=4,'hd'=4] {'hd'}, dimensions={0}, use_global_device_ids=true | all-gather | bytes 327680 | tf_op jit(solution)/shard_map/all_gather | solution.py:198
  238.3 7.7 while.156
  247.1 12.9 all-gather.1
  260.0 6.8 while.157
  289.1 14.6 all-to-all-start.5
  313.3 7.6 while.154
  321.9 11.6 all-gather
  336.4 6.8 while.155
  343.1 7.1 fusion.101
  369.2 5.5 all-to-all-start.2
  376.4 6.3 while.152
  393.6 7.3 multiply_reduce_fusion.19
  401.5 9.2 multiply_reduce_fusion.13
  410.8 7.1 multiply_reduce_fusion.18
  418.0 9.1 multiply_convert_fusion.3
  434.2 5.1 all-to-all-start.9
  446.5 13.0 all-to-all-done.9
  472.3 10.0 all-gather.3
  495.6 7.8 while.153
  509.5 6.3 fusion.53
  524.5 12.2 all-gather.2
  553.0 6.8 while.151
  565.2 6.4 fusion.51
  580.1 6.3 reduce-window.70
  603.2 6.2 reduce-window.76
  637.2 6.4 fusion.116
  653.0 6.3 fusion.109
  675.4 5.2 all-to-all-start.7
  708.2 16.6 %reduce-scatter.5.cloned.1.call-done = bf16[128,256]{1,0:T(8,128)(2,1)} async-done(((bf16[512,256]{1,0:T(8,128)(2,1)}), bf16[128,256]{1,0:T(8,128)(2,1)}) %reduce-scatter.5.cloned.1.call-update) | async-done | bytes 65552 | tf_op jit(solution)/shard_map/reduce_scatter | solution.py:323
  724.8 6.5 multiply_reduce_fusion.9
  741.9 19.9 %fusion.38 = f32[1536,6448]{1,0:T(8,128)} fusion(bf16[128,48]{1,0:T(8,128)(2,1)S(1)} %copy.500, bf16[128,3328]{1,0:T(8,128)(2,1)S(1)} %fusion.98, bf16[128,3072]{1,0:T(8,128)(2,1)S(1)} %copy-done.28, bf16[128,48]{1,0:T(8,128)(2,1)S(1)} %copy-done.103, bf16[128,3328]{1,0:T(8,128)(2,1)S(1)} %fusion.99, bf16[128,3072]{1,0:T(8,128)(2,1)} %get-tuple-element.1175, ...), kind=kOutput, calls=%fused_computation.78 | convolution fusion | flops 5092294656 | bytes 43704320 | tf_op jit(solution)/shard_map/dot_general | solution.py:372
  764.4 7.0 fusion.278
  771.4 9.5 fusion.276
  788.5 8.9 convolution_add_fusion.2
  798.7 9.0 convolution_add_fusion.3
  809.9 11.9 fusion.118
  821.8 6.1 fusion.84
  828.0 5.1 fusion.85
  836.5 293.6 %reduce-scatter.9.cloned.1.call-done = f32[48,6448]{1,0:T(8,128)} async-done(((f32[1536,6448]{1,0:T(8,128)}), f32[48,6448]{1,0:T(8,128)}) %reduce-scatter.9.cloned.1.call-update) | async-done | bytes 1238032 | tf_op jit(solution)/shard_map/reduce_scatter | solution.py:371
  1135.3 125.0 %all-reduce.31.cloned.1.call-done = (f32[1536]{0:T(1024)}, f32[4,3328]{1,0:T(4,128)}, f32[3328]{0:T(1024)}, f32[48]{0:T(128)}, f32[48]{0:T(128)}, /*index=5*/f32[48]{0:T(128)}, f32[3072]{0:T(1024)}) async-done(((f32[1536]{0:T(1024)}, f32[4,3328]{1,0:T(4,128)}, f32[3328]{0:T(1024)}, f32[48]{0:T(128)}, f32[48]{0:T(128)}, /*index=5*/f32[48]{0:T(128)}, f32[3072]{0:T(1024)}), (f32[1536]{0:T(1024)}, ...) | async-done | bytes 85584 | tf_op jit(solution)/shard_map/psum | solution.py:388
  1260.2 214.8 %reduce-scatter.11.cloned.1.call-done = f32[96,1536]{1,0:T(8,128)} async-done(((f32[3072,1536]{1,0:T(8,128)}), f32[96,1536]{1,0:T(8,128)}) %reduce-scatter.11.cloned.1.call-update) | async-done | bytes 589840 | tf_op jit(solution)/shard_map/reduce_scatter | solution.py:380
  (830 shorter events, 433.9 us)
Async XLA Ops:
  7.2 80.4 %copy-start.12 = (bf16[2,128,1536]{2,1,0:T(8,128)(2,1)S(1)}, bf16[2,128,1536]{2,1,0:T(8,128)(2,1)}, u32[]{:S(2)}) copy-start(bf16[2,128,1536]{2,1,0:T(8,128)(2,1)} %param.35) | copy-start | bytes 2359300
  7.2 80.4 %copy-start.127 = (f32[1536]{0:T(1024)S(1)}, f32[1536]{0:T(1024)}, u32[]{:S(2)}) copy-start(f32[1536]{0:T(1024)} %param.37) | copy-start | bytes 18436
  7.2 145.4 %all-gather.10.cloned.1.call-start = ((), (), s32[]{:S(2)}) async-start(), calls=%async_computation.16 | async-start | bytes 10543104 | tf_op jit(solution)/shard_map/all_gather | solution.py:162
  7.9 385.7 %all-gather.12.cloned.1.call-start = ((), (), s32[]{:S(2)}) async-start(), calls=%async_computation.17 | async-start | bytes 9732096 | tf_op jit(solution)/shard_map/all_gather | solution.py:161
  87.8 64.8 %copy-start.18 = (bf16[128,1536]{1,0:T(8,128)(2,1)}, bf16[128,1536]{1,0:T(8,128)(2,1)S(1)}, u32[]{:S(2)}) copy-start(bf16[128,1536]{1,0:T(8,128)(2,1)S(1)} %get-tuple-element.1191) | copy-start | bytes 1179652
  87.8 74.5 %copy-start.15 = (bf16[128,1536]{1,0:T(8,128)(2,1)}, bf16[128,1536]{1,0:T(8,128)(2,1)S(1)}, u32[]{:S(2)}) copy-start(bf16[128,1536]{1,0:T(8,128)(2,1)S(1)} %get-tuple-element.1190) | copy-start | bytes 1179652
  88.8 16.4 %all-to-all-start.4 = ((bf16[128,4,12]{0,2,1:T(8,128)(2,1)}), bf16[128,4,12]{0,2,1:T(8,128)(2,1)S(1)}, u32[]{:S(2)}, u32[]{:S(2)}) async-start(bf16[128,4,12]{0,2,1:T(8,128)(2,1)} %all_to_all.141), calls=%async_computation.4 | async-start | bytes 32768 | tf_op jit(solution)/shard_map/all_to_all | solution.py:196
  92.1 309.4 %all-gather.14.cloned.1.call-start = ((), (), s32[]{:S(2)}) async-start(), calls=%async_computation.18 | async-start | bytes 9732096 | tf_op jit(solution)/shard_map/all_gather | solution.py:164
  97.3 84.5 %copy-start.80 = (f32[3328]{0:T(1024)}, f32[3328]{0:T(1024)S(1)}, u32[]{:S(2)}) copy-start(f32[3328]{0:T(1024)S(1)} %get-tuple-element.1033) | copy-start | bytes 39940
  101.0 47.9 %copy-start.121 = (f32[2,256]{1,0:T(2,128)}, f32[2,256]{1,0:T(2,128)S(1)}, u32[]{:S(2)}) copy-start(f32[2,256]{1,0:T(2,128)S(1)} %get-tuple-element.1240) | copy-start | bytes 6148
  101.0 47.9 %copy-start.137 = (f32[2,256]{1,0:T(2,128)}, f32[2,256]{1,0:T(2,128)S(1)}, u32[]{:S(2)}) copy-start(f32[2,256]{1,0:T(2,128)S(1)} %get-tuple-element.1241) | copy-start | bytes 6148
  102.4 46.4 %copy-start.136 = (f32[2,256]{1,0:T(2,128)}, f32[2,256]{1,0:T(2,128)S(1)}, u32[]{:S(2)}) copy-start(f32[2,256]{1,0:T(2,128)S(1)} %get-tuple-element.1247) | copy-start | bytes 6148
  104.0 44.9 %copy-start.157 = (f32[12]{0:T(128)}, f32[12]{0:T(128)S(1)}, u32[]{:S(2)}) copy-start(f32[12]{0:T(128)S(1)} %dynamic_slice.178) | copy-start | bytes 148
  105.2 10.8 all-to-all-start.1
  116.1 25.5 %copy-start.78 = (f32[2,8,4,128]{3,1,2,0:T(8,128)}, f32[2,8,4,128]{3,1,2,0:T(8,128)S(1)}, u32[]{:S(2)}) copy-start(f32[2,8,4,128]{3,1,2,0:T(8,128)S(1)} %copy.565) | copy-start | bytes 98308
  116.1 25.5 %copy-start.79 = (f32[2,8,4,128]{3,1,2,0:T(8,128)}, f32[2,8,4,128]{3,1,2,0:T(8,128)S(1)}, u32[]{:S(2)}) copy-start(f32[2,8,4,128]{3,1,2,0:T(8,128)S(1)} %copy.563) | copy-start | bytes 98308
  116.2 33.4 %copy-start.63 = (f32[2,256,12]{1,0,2:T(2,128)}, f32[2,256,12]{1,0,2:T(2,128)S(1)}, u32[]{:S(2)}) copy-start(f32[2,256,12]{1,0,2:T(2,128)S(1)} %reshape.754) | copy-start | bytes 73732
  116.3 33.4 %copy-start.61 = (f32[2,256,12]{1,0,2:T(2,128)}, f32[2,256,12]{1,0,2:T(2,128)S(1)}, u32[]{:S(2)}) copy-start(f32[2,256,12]{1,0,2:T(2,128)S(1)} %reshape.763) | copy-start | bytes 73732
  118.6 40.6 %copy-start.93 = (f32[2,12,256]{2,1,0:T(8,128)}, f32[2,12,256]{2,1,0:T(8,128)S(1)}, u32[]{:S(2)}) copy-start(f32[2,12,256]{2,1,0:T(8,128)S(1)} %reshape.833) | copy-start | bytes 73732
  120.4 38.8 %copy-start.134 = (f32[2,12]{1,0:T(2,128)}, f32[2,12]{1,0:T(2,128)S(1)}, u32[]{:S(2)}) copy-start(f32[2,12]{1,0:T(2,128)S(1)} %slice_reduce_fusion.10) | copy-start | bytes 292
  122.0 37.3 %copy-start.59 = (f32[2,12,256]{2,1,0:T(8,128)}, f32[2,12,256]{2,1,0:T(8,128)S(1)}, u32[]{:S(2)}) copy-start(f32[2,12,256]{2,1,0:T(8,128)S(1)} %reshape.841) | copy-start | bytes 73732
  122.1 37.1 %copy-start.132 = (f32[2,12]{1,0:T(2,128)}, f32[2,12]{1,0:T(2,128)S(1)}, u32[]{:S(2)}) copy-start(f32[2,12]{1,0:T(2,128)S(1)} %slice_reduce_fusion.8) | copy-start | bytes 292
  123.7 35.6 %copy-start.94 = (f32[2,12,256]{2,1,0:T(8,128)}, f32[2,12,256]{2,1,0:T(8,128)S(1)}, u32[]{:S(2)}) copy-start(f32[2,12,256]{2,1,0:T(8,128)S(1)} %reshape.835) | copy-start | bytes 73732
  141.6 17.7 %copy-start.74 = (f32[512,12]{0,1:T(8,128)}, f32[512,12]{0,1:T(8,128)S(1)}, u32[]{:S(2)}) copy-start(f32[512,12]{0,1:T(8,128)S(1)} %multiply_bitcast_fusion.5) | copy-start | bytes 73732
  159.3 7.4 collective-permute-start.1
  164.6 15.9 %collective-permute-start = (bf16[3,3328]{1,0:T(4,128)(2,1)}, bf16[3,3328]{1,0:T(4,128)(2,1)S(1)}, u32[]{:S(2)}, u32[]{:S(2)}) collective-permute-start(bf16[3,3328]{1,0:T(4,128)(2,1)} %slice.380), channel_id=1, source_target_pairs={{0,1},{1,2},{2,3},{3,4},{4,5},{5,6},{6,7},{7,8},{8,9},{9,10},{10,1... | collective-permute-start | bytes 59912 | tf_op jit(solution)/shard_map/ppermute | solution.py:19
  173.7 50.4 %all-to-all-start.3 = ((bf16[128,4,768]{0,2,1:T(8,128)(2,1)}), bf16[128,4,768]{0,2,1:T(8,128)(2,1)}, u32[]{:S(2)}, u32[]{:S(2)}) async-start(bf16[128,4,768]{0,2,1:T(8,128)(2,1)} %bitcast.581), calls=%async_computation.3 | async-start | bytes 1572864 | tf_op jit(solution)/shard_map/all_to_all | solution.py:195
  206.4 16.7 %copy-start.54 = (bf16[512,256]{1,0:T(8,128)(2,1)}, bf16[512,256]{1,0:T(8,128)(2,1)S(1)}, u32[]{:S(2)}) copy-start(bf16[512,256]{1,0:T(8,128)(2,1)S(1)} %all_gather.74) | copy-start | bytes 786436
  224.1 64.9 %all-to-all-start = ((bf16[128,4,768]{0,2,1:T(8,128)(2,1)}), bf16[128,4,768]{0,2,1:T(8,128)(2,1)}, u32[]{:S(2)}, u32[]{:S(2)}) async-start(bf16[128,4,768]{0,2,1:T(8,128)(2,1)} %bitcast.579), calls=%async_computation | async-start | bytes 1572864 | tf_op jit(solution)/shard_map/all_to_all | solution.py:195
  289.1 80.1 %all-to-all-start.5 = ((bf16[4,128,768]{1,2,0:T(8,128)(2,1)}), bf16[4,128,768]{1,2,0:T(8,128)(2,1)}, u32[]{:S(2)}, u32[]{:S(2)}) async-start(bf16[4,128,768]{1,2,0:T(8,128)(2,1)} %copy.441), calls=%async_computation.5 | async-start | bytes 1572864 | tf_op jit(solution)/shard_map/all_to_all | solution.py:221
  369.2 18.9 %all-to-all-start.2 = ((bf16[4,128,768]{1,2,0:T(8,128)(2,1)}), bf16[4,128,768]{1,2,0:T(8,128)(2,1)}, u32[]{:S(2)}, u32[]{:S(2)}) async-start(bf16[4,128,768]{1,2,0:T(8,128)(2,1)} %copy.425), calls=%async_computation.2 | async-start | bytes 1572864 | tf_op jit(solution)/shard_map/all_to_all | solution.py:221
  401.5 16.5 %slice-start = ((s8[9437184]{0:T(1024)(128)(4,1)}), s8[4194304]{0:T(1024)(128)(4,1)S(1)}, s32[]{:S(2)}) async-start(s8[9437184]{0:T(1024)(128)(4,1)} %bitcast.551), calls=%async_computation.24 | async-start | bytes 8388608
  401.5 16.5 %slice-start.1 = ((s8[9437184]{0:T(1024)(128)(4,1)}), s8[4194304]{0:T(1024)(128)(4,1)S(1)}, s32[]{:S(2)}) async-start(s8[9437184]{0:T(1024)(128)(4,1)} %bitcast.551), calls=%async_computation.25 | async-start | bytes 8388608
  434.2 25.3 %all-to-all-start.9 = ((bf16[128,4,768]{0,2,1:T(8,128)(2,1)}), bf16[128,4,768]{0,2,1:T(8,128)(2,1)}, u32[]{:S(2)}, u32[]{:S(2)}) async-start(bf16[128,4,768]{0,2,1:T(8,128)(2,1)} %bitcast.580), calls=%async_computation.10 | async-start | bytes 1572864 | tf_op jit(solution)/shard_map/all_to_all | solution.py:282
  444.2 20.7 %copy-start.180 = (f32[2,12,1,1]{1,3,2,0:T(1,128)}, f32[2,12,1,1]{1,3,2,0:T(1,128)S(1)}, u32[]{:S(2)}) copy-start(f32[2,12,1,1]{1,3,2,0:T(1,128)S(1)} %get-tuple-element.1855) | copy-start | bytes 292
  459.5 56.3 %all-to-all-start.6 = ((bf16[128,4,768]{0,2,1:T(8,128)(2,1)}), bf16[128,4,768]{0,2,1:T(8,128)(2,1)}, u32[]{:S(2)}, u32[]{:S(2)}) async-start(bf16[128,4,768]{0,2,1:T(8,128)(2,1)} %bitcast.84), calls=%async_computation.6 | async-start | bytes 1572864 | tf_op jit(solution)/shard_map/all_to_all | solution.py:282
  571.6 65.6 %copy-start.22 = (bf16[2,256,12,64]{1,0,3,2:T(2,128)(2,1)S(1)}, bf16[2,256,12,64]{1,0,3,2:T(2,128)(2,1)}, u32[]{:S(2)}) copy-start(bf16[2,256,12,64]{1,0,3,2:T(2,128)(2,1)} %all_to_all.156) | copy-start | bytes 2359300
  620.8 12.0 all-to-all-start.11
  632.9 15.1 %all-to-all-start.8 = ((bf16[4,128,12]{1,2,0:T(8,128)(2,1)}), bf16[4,128,12]{1,2,0:T(8,128)(2,1)}, u32[]{:S(2)}, u32[]{:S(2)}) async-start(bf16[4,128,12]{1,2,0:T(8,128)(2,1)} %copy.470), calls=%async_computation.9 | async-start | bytes 32768 | tf_op jit(solution)/shard_map/all_to_all | solution.py:319
  648.0 27.4 %all-to-all-start.10 = ((bf16[4,128,768]{1,2,0:T(8,128)(2,1)}), bf16[4,128,768]{1,2,0:T(8,128)(2,1)}, u32[]{:S(2)}, u32[]{:S(2)}) async-start(bf16[4,128,768]{1,2,0:T(8,128)(2,1)} %copy.484), calls=%async_computation.11 | async-start | bytes 1572864 | tf_op jit(solution)/shard_map/all_to_all | solution.py:316
  675.4 21.7 %all-to-all-start.7 = ((bf16[4,128,768]{1,2,0:T(8,128)(2,1)}), bf16[4,128,768]{1,2,0:T(8,128)(2,1)}, u32[]{:S(2)}, u32[]{:S(2)}) async-start(bf16[4,128,768]{1,2,0:T(8,128)(2,1)} %copy.456), calls=%async_computation.7 | async-start | bytes 1572864 | tf_op jit(solution)/shard_map/all_to_all | solution.py:316
  680.6 23.5 %reduce-scatter.7.cloned.1.call-start = ((), (), s32[]{:S(2)}) async-start(), calls=%async_computation.20 | async-start | bytes 327680 | tf_op jit(solution)/shard_map/reduce_scatter | solution.py:323
  683.6 41.1 %reduce-scatter.5.cloned.1.call-start = ((), (), s32[]{:S(2)}) async-start(), calls=%async_computation.19 | async-start | bytes 327680 | tf_op jit(solution)/shard_map/reduce_scatter | solution.py:323
  692.4 437.6 %reduce-scatter.9.cloned.1.call-start = ((), (), s32[]{:S(2)}) async-start(), calls=%async_computation.21 | async-start | bytes 41361408 | tf_op jit(solution)/shard_map/reduce_scatter | solution.py:371
  733.4 5.8 collective-permute-start.3
  735.3 6.4 collective-permute-start.2
  761.8 498.5 %all-reduce.31.cloned.1.call-start = ((), (), s32[]{:S(2)}) async-start(), calls=%async_computation.23 | async-start | bytes 183296 | tf_op jit(solution)/shard_map/psum | solution.py:388
  809.9 665.2 %reduce-scatter.11.cloned.1.call-start = ((), (), s32[]{:S(2)}) async-start(), calls=%async_computation.22 | async-start | bytes 19464192 | tf_op jit(solution)/shard_map/reduce_scatter | solution.py:380
  (166 other events, 912.3 us)
Sparse Core Ops, SparseCore 0:
  10.8 90.7 all-gather.9
  104.4 90.3 all-gather.11
  197.6 94.1 all-gather.13
  683.9 20.1 reduce-scatter.6
  706.8 17.8 reduce-scatter.4
  761.9 368.0 reduce-scatter.8
  1137.6 122.5 all-reduce.30
  1267.2 207.8 reduce-scatter.10
where the time goes:
time: 1500 us; the launch traced here: 1490 us
  waiting for transfers between devices  684 us (46%)
  matrix products  216 us (14%)
  local copies, waits for them, and re-layouts  179 us (12%)
  blocking collectives  177 us (12%)
  other arithmetic  140 us (9%)
  starting transfers between devices  77 us (5%)
  between operations  17.4 us (1%)
    reduce_scatter x1, waiting for transfers between devices, shards(): lax.psum_scatter(lax.dot_general(part, proj_all, (((0,), (0,)), ((), ()))...  294 us
    reduce_scatter x1, waiting for transfers between devices, shards(): lax.psum_scatter(lax.dot_general(part, cot_all, (((0,), (0,)), ((), ())),...  215 us
    psum x1, waiting for transfers between devices, shards(): lax.psum((norm_total, taps_total, cbias_total, dtb_total, alog_total, ski...  125 us
    all_gather x1, blocking collectives, fetch(): lax.all_gather(dt_proj, ('dp', 'ctx', 'hd'), axis=0, tiled=True)  76.8 us
    all_gather x6, blocking collectives, carried_in(): lax.all_gather(part.astype(kind), axis)  67.1 us
    dot_general x8, matrix products, back_dot(): lax.dot_general(grad_val, weight, (((1,), (1,)), ((), ())), preferred_ele...  54.5 us
    dot_general x6, matrix products, block_ssd(): y_part = jnp.einsum('ctsh,cshp->cthp', mix_w, x_groups, precision=HIGH)  37.6 us
    all_gather x2, blocking collectives, shards(): bc_all = lax.all_gather(bc_low, 'hd', axis=0, tiled=True)  32.6 us
  transfers between devices with their start and end apart: 24, of which 10 were waited for; matrix products, arithmetic and copies ran while one was open for 24% of the time, Pallas kernels for 0%

commit v1 on v0

--- a/solution.py
+++ b/solution.py
@@ -279,9 +279,20 @@
         d_gated = back_dot(cot_low, out_weight)
         unused, tail_pull = jax.vjp(gate_tail, y_float, gate_in, gate_norm)
         d_mixer, d_gate_in, d_gain = tail_pull(d_gated)
-        d_mixer_heads = lax.all_to_all(
-            d_mixer.astype(jnp.bfloat16), "hd", split_axis=1, concat_axis=0, tiled=True
-        )
+        shard_2 = d_mixer.astype(jnp.bfloat16)
+        ways, here = (lax.axis_size("hd"), lax.axis_index("hd"))
+        width_2 = shard_2.shape[1] // ways
+        dims = list(shard_2.shape)
+        dims[1] = width_2
+        height = dims[0]
+        dims[0] = height * ways
+        full = jnp.zeros(dims, shard_2.dtype)
+        for mask_2 in range(ways):
+            part_2 = lax.dynamic_slice_in_dim(shard_2, (here ^ mask_2) * width_2, width_2, axis=1)
+            if mask_2:
+                part_2 = lax.ppermute(part_2, "hd", [(d, d ^ mask_2) for d in range(ways)])
+            full = lax.dynamic_update_slice_in_dim(full, part_2, (here ^ mask_2) * height, axis=0)
+        d_mixer_heads = full
         d_y_float = d_mixer_heads.astype(jnp.float32)
         d_local = jnp.einsum(
             "th,thp,tn->hpn",

time: 1500 us -> 1460 us (0.973)
  local copies, waits for them, and re-layouts: 179 us -> 150 us
    all_to_all x6 -> x0, local copies, waits for them, and re-layouts: 15.9 us -> none  [shards(): lax.all_to_all(d_mixer.astype(jnp.bfloat16), 'hd', split_axis=1, concat_a...]
  transfers between devices with their start and end apart: 24 -> 28, of which waited for: 10 -> 10; matrix products, arithmetic and copies ran while one was open for 24% -> 22% of each run, Pallas kernels for 0% -> 0%
where the time goes in v1:
time: 1460 us; the launch traced here: 1450 us
  waiting for transfers between devices  683 us (47%)
  matrix products  213 us (15%)
  blocking collectives  180 us (12%)
  local copies, waits for them, and re-layouts  150 us (10%)
  other arithmetic  128 us (9%)
  starting transfers between devices  76.1 us (5%)
  between operations  17.6 us (1%)
    reduce_scatter x1, waiting for transfers between devices, shards(): lax.psum_scatter(lax.dot_general(part, proj_all, (((0,), (0,)), ((), ()))...  293 us
    reduce_scatter x1, waiting for transfers between devices, shards(): lax.psum_scatter(lax.dot_general(part, cot_all, (((0,), (0,)), ((), ())),...  215 us
    psum x1, waiting for transfers between devices, shards(): lax.psum((norm_total, taps_total, cbias_total, dtb_total, alog_total, ski...  125 us
    all_gather x1, blocking collectives, fetch(): lax.all_gather(dt_proj, ('dp', 'ctx', 'hd'), axis=0, tiled=True)  76.8 us
    all_gather x6, blocking collectives, carried_in(): lax.all_gather(part.astype(kind), axis)  65.9 us
    dot_general x8, matrix products, back_dot(): lax.dot_general(grad_val, weight, (((1,), (1,)), ((), ())), preferred_ele...  55.4 us
    dot_general x6, matrix products, block_ssd(): y_part = jnp.einsum('ctsh,cshp->cthp', mix_w, x_groups, precision=HIGH)  40.1 us
    all_gather x2, blocking collectives, shards(): bc_all = lax.all_gather(bc_low, 'hd', axis=0, tiled=True)  36.9 us
  transfers between devices with their start and end apart: 28, of which 10 were waited for; matrix products, arithmetic and copies ran while one was open for 22% of the time, Pallas kernels for 0%

profile of v1, /device:TPU:0, one launch (start us, length us, event | category | flops | bytes accessed | tf_op | source)
XLA Modules:
  0.0 1447.9 jit_solution(12907728612788583242)
XLA Ops:
  8.7 76.8 %all_gather.68 = bf16[1536,48]{1,0:T(8,128)(2,1)S(1)} all-gather(bf16[48,48]{1,0:T(8,128)(2,1)} %param.40), channel_id=1, replica_groups=mesh['dp'=2,'ctx'=4,'hd'=4] {'dp','ctx','hd'}, dimensions={0}, use_global_device_ids=true | all-gather | bytes 152064 | tf_op jit(solution)/shard_map/all_gather | solution.py:163
  104.8 5.0 all-to-all-start.1
  109.9 5.6 all-to-all-done.1
  125.0 14.3 all-gather.5
  141.6 6.4 all-gather.4
  153.8 5.6 convolution_convert_fusion
  173.0 5.4 all-to-all-start.3
  184.4 21.9 %all_gather.74 = bf16[512,256]{1,0:T(8,128)(2,1)S(1)} all-gather(bf16[128,256]{1,0:T(8,128)(2,1)S(1)} %slice.403), channel_id=1, replica_groups=mesh['dp'=2,'ctx'=4,'hd'=4] {'hd'}, dimensions={0}, use_global_device_ids=true | all-gather | bytes 327680 | tf_op jit(solution)/shard_map/all_gather | solution.py:198
  206.3 15.0 %all_gather.33 = bf16[512,256]{1,0:T(8,128)(2,1)S(1)} all-gather(bf16[128,256]{1,0:T(8,128)(2,1)S(1)} %slice.386), channel_id=1, replica_groups=mesh['dp'=2,'ctx'=4,'hd'=4] {'hd'}, dimensions={0}, use_global_device_ids=true | all-gather | bytes 327680 | tf_op jit(solution)/shard_map/all_gather | solution.py:198
  238.0 7.7 while.156
  246.7 11.8 all-gather.1
  258.5 7.0 while.157
  287.7 14.5 %all-to-all-start.5 = ((bf16[4,128,768]{1,2,0:T(8,128)(2,1)}), bf16[4,128,768]{1,2,0:T(8,128)(2,1)}, u32[]{:S(2)}, u32[]{:S(2)}) async-start(bf16[4,128,768]{1,2,0:T(8,128)(2,1)} %copy.489), calls=%async_computation.5 | async-start | bytes 1572864 | tf_op jit(solution)/shard_map/all_to_all | solution.py:221
  311.3 7.7 while.154
  320.1 11.6 all-gather
  333.7 7.0 while.155
  340.7 7.3 fusion.97
  366.9 5.3 all-to-all-start.2
  373.9 6.3 while.152
  391.0 7.3 multiply_reduce_fusion.19
  398.9 9.2 multiply_reduce_fusion.13
  408.2 7.1 multiply_reduce_fusion.18
  415.4 9.1 multiply_convert_fusion.3
  448.7 7.5 collective-permute-done.7
  473.7 10.7 all-gather.3
  495.1 7.8 while.153
  515.9 11.2 all-gather.2
  549.5 7.4 fusion.51
  563.4 7.6 fusion.53
  578.9 5.2 all-to-all-start.9
  593.0 6.5 fusion.112
  606.6 5.4 all-to-all-start.8
  612.1 6.4 fusion.113
  633.2 5.1 all-to-all-start.6
  653.6 8.2 reduce-scatter.7.cloned.1.call-done
  666.1 16.4 %reduce-scatter.5.cloned.1.call-done = bf16[128,256]{1,0:T(8,128)(2,1)} async-done(((bf16[512,256]{1,0:T(8,128)(2,1)}), bf16[128,256]{1,0:T(8,128)(2,1)}) %reduce-scatter.5.cloned.1.call-update) | async-done | bytes 65552 | tf_op jit(solution)/shard_map/reduce_scatter | solution.py:334
  682.6 5.8 multiply_reduce_fusion.9
  698.8 19.9 %fusion.38 = f32[1536,6448]{1,0:T(8,128)} fusion(bf16[128,48]{1,0:T(8,128)(2,1)S(1)} %copy.558, bf16[128,3328]{1,0:T(8,128)(2,1)S(1)} %fusion.94, bf16[128,3072]{1,0:T(8,128)(2,1)S(1)} %copy-done.27, bf16[128,48]{1,0:T(8,128)(2,1)S(1)} %copy.557, bf16[128,3328]{1,0:T(8,128)(2,1)S(1)} %fusion.95, bf16[128,3072]{1,0:T(8,128)(2,1)} %get-tuple-element.1175, ...), kind=kOutput, calls=%fused_computation.78 | convolution fusion | flops 5092294656 | bytes 43704320 | tf_op jit(solution)/shard_map/dot_general | solution.py:383
  721.3 7.9 fusion.272
  729.2 9.6 fusion.270
  745.5 8.9 convolution_add_fusion.2
  755.8 8.9 convolution_add_fusion.3
  767.0 12.1 fusion.106
  779.1 6.0 fusion.84
  785.1 5.1 fusion.85
  793.6 293.1 %reduce-scatter.9.cloned.1.call-done = f32[48,6448]{1,0:T(8,128)} async-done(((f32[1536,6448]{1,0:T(8,128)}), f32[48,6448]{1,0:T(8,128)}) %reduce-scatter.9.cloned.1.call-update) | async-done | bytes 1238032 | tf_op jit(solution)/shard_map/reduce_scatter | solution.py:382
  1091.9 125.0 %all-reduce.31.cloned.1.call-done = (f32[1536]{0:T(1024)}, f32[4,3328]{1,0:T(4,128)}, f32[3328]{0:T(1024)}, f32[48]{0:T(128)}, f32[48]{0:T(128)}, /*index=5*/f32[48]{0:T(128)}, f32[3072]{0:T(1024)}) async-done(((f32[1536]{0:T(1024)}, f32[4,3328]{1,0:T(4,128)}, f32[3328]{0:T(1024)}, f32[48]{0:T(128)}, f32[48]{0:T(128)}, /*index=5*/f32[48]{0:T(128)}, f32[3072]{0:T(1024)}), (f32[1536]{0:T(1024)}, ...) | async-done | bytes 85584 | tf_op jit(solution)/shard_map/psum | solution.py:399
  1216.9 214.8 %reduce-scatter.11.cloned.1.call-done = f32[96,1536]{1,0:T(8,128)} async-done(((f32[3072,1536]{1,0:T(8,128)}), f32[96,1536]{1,0:T(8,128)}) %reduce-scatter.11.cloned.1.call-update) | async-done | bytes 589840 | tf_op jit(solution)/shard_map/reduce_scatter | solution.py:391
  (811 shorter events, 391.6 us)
Async XLA Ops:
  7.2 79.9 %copy-start.18 = (bf16[2,128,1536]{2,1,0:T(8,128)(2,1)S(1)}, bf16[2,128,1536]{2,1,0:T(8,128)(2,1)}, u32[]{:S(2)}) copy-start(bf16[2,128,1536]{2,1,0:T(8,128)(2,1)} %param.35) | copy-start | bytes 2359300
  7.2 79.9 %copy-start.103 = (f32[1536]{0:T(1024)S(1)}, f32[1536]{0:T(1024)}, u32[]{:S(2)}) copy-start(f32[1536]{0:T(1024)} %param.37) | copy-start | bytes 18436
  7.2 146.6 %all-gather.10.cloned.1.call-start = ((), (), s32[]{:S(2)}) async-start(), calls=%async_computation.14 | async-start | bytes 10543104 | tf_op jit(solution)/shard_map/all_gather | solution.py:162
  7.9 383.1 %all-gather.12.cloned.1.call-start = ((), (), s32[]{:S(2)}) async-start(), calls=%async_computation.15 | async-start | bytes 9732096 | tf_op jit(solution)/shard_map/all_gather | solution.py:161
  87.6 66.1 %copy-start.24 = (bf16[128,1536]{1,0:T(8,128)(2,1)}, bf16[128,1536]{1,0:T(8,128)(2,1)S(1)}, u32[]{:S(2)}) copy-start(bf16[128,1536]{1,0:T(8,128)(2,1)S(1)} %get-tuple-element.1191) | copy-start | bytes 1179652
  87.6 75.6 %copy-start.21 = (bf16[128,1536]{1,0:T(8,128)(2,1)}, bf16[128,1536]{1,0:T(8,128)(2,1)S(1)}, u32[]{:S(2)}) copy-start(bf16[128,1536]{1,0:T(8,128)(2,1)S(1)} %get-tuple-element.1190) | copy-start | bytes 1179652
  88.6 16.3 %all-to-all-start.4 = ((bf16[128,4,12]{0,2,1:T(8,128)(2,1)}), bf16[128,4,12]{0,2,1:T(8,128)(2,1)S(1)}, u32[]{:S(2)}, u32[]{:S(2)}) async-start(bf16[128,4,12]{0,2,1:T(8,128)(2,1)} %all_to_all.113), calls=%async_computation.4 | async-start | bytes 32768 | tf_op jit(solution)/shard_map/all_to_all | solution.py:196
  91.8 307.0 %all-gather.14.cloned.1.call-start = ((), (), s32[]{:S(2)}) async-start(), calls=%async_computation.16 | async-start | bytes 9732096 | tf_op jit(solution)/shard_map/all_gather | solution.py:164
  97.0 82.8 %copy-start.74 = (f32[3328]{0:T(1024)}, f32[3328]{0:T(1024)S(1)}, u32[]{:S(2)}) copy-start(f32[3328]{0:T(1024)S(1)} %get-tuple-element.1033) | copy-start | bytes 39940
  101.9 46.8 %copy-start.99 = (f32[2,256]{1,0:T(2,128)}, f32[2,256]{1,0:T(2,128)S(1)}, u32[]{:S(2)}) copy-start(f32[2,256]{1,0:T(2,128)S(1)} %get-tuple-element.1248) | copy-start | bytes 6148
  101.9 46.8 %copy-start.115 = (f32[2,256]{1,0:T(2,128)}, f32[2,256]{1,0:T(2,128)S(1)}, u32[]{:S(2)}) copy-start(f32[2,256]{1,0:T(2,128)S(1)} %get-tuple-element.1249) | copy-start | bytes 6148
  102.0 46.7 %copy-start.113 = (f32[2,256]{1,0:T(2,128)}, f32[2,256]{1,0:T(2,128)S(1)}, u32[]{:S(2)}) copy-start(f32[2,256]{1,0:T(2,128)S(1)} %get-tuple-element.1255) | copy-start | bytes 6148
  103.6 45.2 %copy-start.138 = (f32[12]{0:T(128)}, f32[12]{0:T(128)S(1)}, u32[]{:S(2)}) copy-start(f32[12]{0:T(128)S(1)} %dynamic_slice.202) | copy-start | bytes 148
  104.8 10.7 all-to-all-start.1
  115.6 25.7 %copy-start.70 = (f32[2,8,4,128]{3,1,2,0:T(8,128)}, f32[2,8,4,128]{3,1,2,0:T(8,128)S(1)}, u32[]{:S(2)}) copy-start(f32[2,8,4,128]{3,1,2,0:T(8,128)S(1)} %copy.621) | copy-start | bytes 98308
  115.7 25.8 %copy-start.72 = (f32[2,8,4,128]{3,1,2,0:T(8,128)}, f32[2,8,4,128]{3,1,2,0:T(8,128)S(1)}, u32[]{:S(2)}) copy-start(f32[2,8,4,128]{3,1,2,0:T(8,128)S(1)} %copy.619) | copy-start | bytes 98308
  115.8 33.7 %copy-start.63 = (f32[2,256,12]{1,0,2:T(2,128)}, f32[2,256,12]{1,0,2:T(2,128)S(1)}, u32[]{:S(2)}) copy-start(f32[2,256,12]{1,0,2:T(2,128)S(1)} %reshape.757) | copy-start | bytes 73732
  115.9 33.7 %copy-start.61 = (f32[2,256,12]{1,0,2:T(2,128)}, f32[2,256,12]{1,0,2:T(2,128)S(1)}, u32[]{:S(2)}) copy-start(f32[2,256,12]{1,0,2:T(2,128)S(1)} %reshape.768) | copy-start | bytes 73732
  118.1 41.2 %copy-start.82 = (f32[2,12,256]{2,1,0:T(8,128)}, f32[2,12,256]{2,1,0:T(8,128)S(1)}, u32[]{:S(2)}) copy-start(f32[2,12,256]{2,1,0:T(8,128)S(1)} %reshape.841) | copy-start | bytes 73732
  120.0 39.4 %copy-start.111 = (f32[2,12]{1,0:T(2,128)}, f32[2,12]{1,0:T(2,128)S(1)}, u32[]{:S(2)}) copy-start(f32[2,12]{1,0:T(2,128)S(1)} %slice_reduce_fusion.10) | copy-start | bytes 292
  121.5 37.8 %copy-start.59 = (f32[2,12,256]{2,1,0:T(8,128)}, f32[2,12,256]{2,1,0:T(8,128)S(1)}, u32[]{:S(2)}) copy-start(f32[2,12,256]{2,1,0:T(8,128)S(1)} %reshape.849) | copy-start | bytes 73732
  121.7 37.7 %copy-start.108 = (f32[2,12]{1,0:T(2,128)}, f32[2,12]{1,0:T(2,128)S(1)}, u32[]{:S(2)}) copy-start(f32[2,12]{1,0:T(2,128)S(1)} %slice_reduce_fusion.8) | copy-start | bytes 292
  123.2 36.1 %copy-start.83 = (f32[2,12,256]{2,1,0:T(8,128)}, f32[2,12,256]{2,1,0:T(8,128)S(1)}, u32[]{:S(2)}) copy-start(f32[2,12,256]{2,1,0:T(8,128)S(1)} %reshape.843) | copy-start | bytes 73732
  159.4 8.8 collective-permute-start.1
  165.5 13.0 collective-permute-start
  173.0 51.1 %all-to-all-start.3 = ((bf16[128,4,768]{2,0,1:T(8,128)(2,1)}), bf16[128,4,768]{2,0,1:T(8,128)(2,1)}, u32[]{:S(2)}, u32[]{:S(2)}) async-start(bf16[128,4,768]{2,0,1:T(8,128)(2,1)} %bitcast.580), calls=%async_computation.3 | async-start | bytes 1572864 | tf_op jit(solution)/shard_map/all_to_all | solution.py:195
  224.1 63.6 %all-to-all-start = ((bf16[128,4,768]{2,0,1:T(8,128)(2,1)}), bf16[128,4,768]{2,0,1:T(8,128)(2,1)}, u32[]{:S(2)}, u32[]{:S(2)}) async-start(bf16[128,4,768]{2,0,1:T(8,128)(2,1)} %bitcast.579), calls=%async_computation | async-start | bytes 1572864 | tf_op jit(solution)/shard_map/all_to_all | solution.py:195
  287.7 79.3 %all-to-all-start.5 = ((bf16[4,128,768]{1,2,0:T(8,128)(2,1)}), bf16[4,128,768]{1,2,0:T(8,128)(2,1)}, u32[]{:S(2)}, u32[]{:S(2)}) async-start(bf16[4,128,768]{1,2,0:T(8,128)(2,1)} %copy.489), calls=%async_computation.5 | async-start | bytes 1572864 | tf_op jit(solution)/shard_map/all_to_all | solution.py:221
  366.9 18.6 %all-to-all-start.2 = ((bf16[4,128,768]{1,2,0:T(8,128)(2,1)}), bf16[4,128,768]{1,2,0:T(8,128)(2,1)}, u32[]{:S(2)}, u32[]{:S(2)}) async-start(bf16[4,128,768]{1,2,0:T(8,128)(2,1)} %copy.473), calls=%async_computation.2 | async-start | bytes 1572864 | tf_op jit(solution)/shard_map/all_to_all | solution.py:221
  431.0 15.9 %collective-permute-start.6 = (bf16[128,768]{1,0:T(8,128)(2,1)}, bf16[128,768]{1,0:T(8,128)(2,1)}, u32[]{:S(2)}, u32[]{:S(2)}) collective-permute-start(bf16[128,768]{1,0:T(8,128)(2,1)} %get-tuple-element.1200), channel_id=1, source_target_pairs={{0,1},{1,0},{2,3},{3,2},{4,5},{5,4},{6,7},{7,6},{8,9},{9,8},{10,11... | collective-permute-start | bytes 589832 | tf_op jit(solution)/shard_map/ppermute | solution.py:293
  438.0 18.2 %collective-permute-start.7 = (bf16[128,768]{1,0:T(8,128)(2,1)}, bf16[128,768]{1,0:T(8,128)(2,1)S(1)}, u32[]{:S(2)}, u32[]{:S(2)}) collective-permute-start(bf16[128,768]{1,0:T(8,128)(2,1)} %get-tuple-element.1199), channel_id=1, source_target_pairs={{0,2},{1,3},{2,0},{3,1},{4,6},{5,7},{6,4},{7,5},{8,10},{9,11},{10,... | collective-permute-start | bytes 589832 | tf_op jit(solution)/shard_map/ppermute | solution.py:293
  440.4 16.5 %collective-permute-start.8 = (bf16[128,768]{1,0:T(8,128)(2,1)}, bf16[128,768]{1,0:T(8,128)(2,1)S(1)}, u32[]{:S(2)}, u32[]{:S(2)}) collective-permute-start(bf16[128,768]{1,0:T(8,128)(2,1)} %get-tuple-element.1198), channel_id=1, source_target_pairs={{0,3},{1,2},{2,1},{3,0},{4,7},{5,6},{6,5},{7,4},{8,11},{9,10},{10,... | collective-permute-start | bytes 589832 | tf_op jit(solution)/shard_map/ppermute | solution.py:293
  442.7 19.8 %collective-permute-start.2 = (bf16[128,768]{1,0:T(8,128)(2,1)}, bf16[128,768]{1,0:T(8,128)(2,1)}, u32[]{:S(2)}, u32[]{:S(2)}) collective-permute-start(bf16[128,768]{1,0:T(8,128)(2,1)} %get-tuple-element.1196), channel_id=1, source_target_pairs={{0,1},{1,0},{2,3},{3,2},{4,5},{5,4},{6,7},{7,6},{8,9},{9,8},{10,11... | collective-permute-start | bytes 589832 | tf_op jit(solution)/shard_map/ppermute | solution.py:293
  443.7 19.8 %collective-permute-start.3 = (bf16[128,768]{1,0:T(8,128)(2,1)}, bf16[128,768]{1,0:T(8,128)(2,1)}, u32[]{:S(2)}, u32[]{:S(2)}) collective-permute-start(bf16[128,768]{1,0:T(8,128)(2,1)} %get-tuple-element.1195), channel_id=1, source_target_pairs={{0,2},{1,3},{2,0},{3,1},{4,6},{5,7},{6,4},{7,5},{8,10},{9,11},{10,... | collective-permute-start | bytes 589832 | tf_op jit(solution)/shard_map/ppermute | solution.py:293
  447.0 17.4 %collective-permute-start.4 = (bf16[128,768]{1,0:T(8,128)(2,1)}, bf16[128,768]{1,0:T(8,128)(2,1)}, u32[]{:S(2)}, u32[]{:S(2)}) collective-permute-start(bf16[128,768]{1,0:T(8,128)(2,1)} %get-tuple-element.1194), channel_id=1, source_target_pairs={{0,3},{1,2},{2,1},{3,0},{4,7},{5,6},{6,5},{7,4},{8,11},{9,10},{10,... | collective-permute-start | bytes 589832 | tf_op jit(solution)/shard_map/ppermute | solution.py:293
  563.4 29.5 %copy-start.89 = (f32[2,256,12]{1,2,0:T(8,128)S(1)}, f32[2,256,12]{1,2,0:T(8,128)}, u32[]{:S(2)}) copy-start(f32[2,256,12]{1,2,0:T(8,128)} %get-tuple-element.1274) | copy-start | bytes 73732
  578.9 10.8 all-to-all-start.9
  589.7 16.9 %all-to-all-start.7 = ((bf16[4,128,12]{1,2,0:T(8,128)(2,1)}), bf16[4,128,12]{1,2,0:T(8,128)(2,1)S(1)}, u32[]{:S(2)}, u32[]{:S(2)}) async-start(bf16[4,128,12]{1,2,0:T(8,128)(2,1)} %copy.523), calls=%async_computation.8 | async-start | bytes 32768 | tf_op jit(solution)/shard_map/all_to_all | solution.py:330
  606.6 26.6 %all-to-all-start.8 = ((bf16[4,128,768]{1,2,0:T(8,128)(2,1)}), bf16[4,128,768]{1,2,0:T(8,128)(2,1)}, u32[]{:S(2)}, u32[]{:S(2)}) async-start(bf16[4,128,768]{1,2,0:T(8,128)(2,1)} %copy.539), calls=%async_computation.9 | async-start | bytes 1572864 | tf_op jit(solution)/shard_map/all_to_all | solution.py:327
  633.2 18.9 %all-to-all-start.6 = ((bf16[4,128,768]{1,2,0:T(8,128)(2,1)}), bf16[4,128,768]{1,2,0:T(8,128)(2,1)}, u32[]{:S(2)}, u32[]{:S(2)}) async-start(bf16[4,128,768]{1,2,0:T(8,128)(2,1)} %copy.506), calls=%async_computation.6 | async-start | bytes 1572864 | tf_op jit(solution)/shard_map/all_to_all | solution.py:327
  638.3 23.5 %reduce-scatter.7.cloned.1.call-start = ((), (), s32[]{:S(2)}) async-start(), calls=%async_computation.18 | async-start | bytes 327680 | tf_op jit(solution)/shard_map/reduce_scatter | solution.py:334
  639.5 43.0 %reduce-scatter.5.cloned.1.call-start = ((), (), s32[]{:S(2)}) async-start(), calls=%async_computation.17 | async-start | bytes 327680 | tf_op jit(solution)/shard_map/reduce_scatter | solution.py:334
  649.5 437.2 %reduce-scatter.9.cloned.1.call-start = ((), (), s32[]{:S(2)}) async-start(), calls=%async_computation.19 | async-start | bytes 41361408 | tf_op jit(solution)/shard_map/reduce_scatter | solution.py:382
  661.8 20.7 %copy-start.128 = (f32[128]{0:T(128)S(1)}, f32[128]{0:T(128)}, u32[]{:S(2)}) copy-start(f32[128]{0:T(128)} %get-tuple-element.1250) | copy-start | bytes 1540
  690.4 5.8 collective-permute-start.9
  692.2 6.4 collective-permute-start.5
  718.7 498.3 %all-reduce.31.cloned.1.call-start = ((), (), s32[]{:S(2)}) async-start(), calls=%async_computation.21 | async-start | bytes 183296 | tf_op jit(solution)/shard_map/psum | solution.py:399
  766.9 664.8 %reduce-scatter.11.cloned.1.call-start = ((), (), s32[]{:S(2)}) async-start(), calls=%async_computation.20 | async-start | bytes 19464192 | tf_op jit(solution)/shard_map/reduce_scatter | solution.py:391
  (152 other events, 960.2 us)
Sparse Core Ops, SparseCore 0:
  10.8 90.7 all-gather.9
  104.4 91.1 all-gather.11
  198.5 93.4 all-gather.13
  641.7 20.1 reduce-scatter.6
  664.6 17.8 reduce-scatter.4
  718.8 367.8 reduce-scatter.8
  1094.3 122.6 all-reduce.30
  1223.9 207.8 reduce-scatter.10
